TPU v7x, 256 devices: a whole 4x4x8 slice. The times are simulated.
256 devices in a mesh: row: 16 (over z, core), col: 8 (over x, y_lo), vec: 2 (over y_hi).
Axes of the slice: x: 4, y: 4 (y_hi: 2, y_lo: 2; y = y_hi * 2 + y_lo), z: 8, core: 2. Of those that a mesh axis runs over, the one named last changes fastest.
Arguments:
- vectors: bfloat16 [16, 131072], P('vec', ('row', 'col')), may hold values from -6 to 6
- tile_vals: bfloat16 [16, 8, 256, 128, 128], P('row', 'col'), may hold values from -0.09375 to 0.09375
- tile_rows: int32 [16, 8, 256], P('row', 'col'), may hold values from 0 to 1023, as said below
- tile_cols: int32 [16, 8, 256], P('row', 'col'), may hold values from 0 to 1023, as said below
- tile_counts: int32 [16, 8], P('row', 'col'), may hold values from 1 to 256, as said below
Outputs:
- product: bfloat16 [16, 131072], P('vec', ('row', 'col'))
- gram: float32 [16, 16], P(None, 'vec')
Inputs may be any that keep to these rules, and one draw needn't show every extreme that they name: `tile_rows`: list [i, j] names tiles whose row index r has i * 64 <= r < (i + 1) * 64 and whose column index c has (c // 8) % (8) == j, that is the column's block of 8 tile rows, numbered c // 8, is held by column group j; live slots name distinct tiles with r >= c; slots at or beyond the count hold in-range indices that must be ignored. `tile_cols`: see tile_rows; the same slots. `tile_counts`: some lists are full in every draw; lists near the top of the triangle hold few tiles.
All inputs are finite; a program needn't handle non-finite values.
Results may differ from a plain program's by a relative error of at most 0.001.
Values may be sent and summed in bfloat16 or wider, within the bound.
A program may use at most 64 MiB of HBM per device.

v0:
```python
import math
import jax
import jax.numpy as jnp
from jax import lax
from jax.sharding import PartitionSpec as P


def shards(vectors, tile_vals, tile_rows, tile_cols, tile_counts):
    nrow = lax.axis_size("row")
    ncol = lax.axis_size("col")
    vlocal, width = vectors.shape
    tile = tile_vals.shape[-1]
    stretch = width // tile
    span = ncol * stretch
    colspan = nrow * stretch
    row_x = lax.all_gather(vectors, "col", axis=1, tiled=True)
    col_x = lax.all_gather(vectors, "row", axis=1, tiled=True)
    tiles = tile_vals[0, 0]
    rows = tile_rows[0, 0]
    cols = tile_cols[0, 0]
    count = tile_counts[0, 0]
    slots = jnp.arange(rows.shape[0], dtype=jnp.int32)
    live = slots < count
    mirror = live & (rows != cols)
    row_place = rows % span
    col_place = cols // span * stretch + cols % stretch
    row_blocks = row_x.reshape(vlocal, span, tile)
    col_blocks = col_x.reshape(vlocal, colspan, tile)
    picked_cols = jnp.take(col_blocks, col_place, axis=1)
    picked_rows = jnp.take(row_blocks, row_place, axis=1)
    down = jnp.einsum("tij,vtj->vti", tiles, picked_cols, preferred_element_type=jnp.float32)
    upper = jnp.einsum("tij,vti->vtj", tiles, picked_rows, preferred_element_type=jnp.float32)
    row_hit = (
        (row_place[None, :] == jnp.arange(span, dtype=jnp.int32)[:, None]) & live[None, :]
    ).astype(jnp.float32)
    col_hit = (
        (col_place[None, :] == jnp.arange(colspan, dtype=jnp.int32)[:, None]) & mirror[None, :]
    ).astype(jnp.float32)
    row_part = jnp.einsum("at,vti->vai", row_hit, down, precision=lax.Precision.HIGHEST).reshape(
        vlocal, span * tile
    )
    col_part = jnp.einsum("at,vti->vai", col_hit, upper, precision=lax.Precision.HIGHEST).reshape(
        vlocal, colspan * tile
    )
    row_whole = lax.psum(row_part, "col")
    col_whole = lax.psum(col_part, "row")
    row_share = lax.dynamic_slice_in_dim(row_whole, lax.axis_index("col") * width, width, 1)
    col_share = lax.dynamic_slice_in_dim(col_whole, lax.axis_index("row") * width, width, 1)
    image = row_share + col_share
    every_vector = lax.all_gather(vectors, "vec", axis=0, tiled=True)
    partial_gram = jnp.dot(
        every_vector.astype(jnp.float32), image.T, precision=lax.Precision.HIGHEST
    )
    gram = lax.psum(partial_gram, ("row", "col")) / math.sqrt(width * nrow * ncol)
    return (image.astype(jnp.bfloat16), gram)


def solution(mesh):
    return jax.shard_map(
        shards,
        mesh=mesh,
        in_specs=(
            P("vec", ("row", "col")),
            P("row", "col", None, None, None),
            P("row", "col", None),
            P("row", "col", None),
            P("row", "col"),
        ),
        out_specs=(P("vec", ("row", "col")), P(None, "vec")),
        check_vma=False,
    )
```

profile of v0, /device:TPU:8, one launch (start us, length us, event | category | flops | bytes accessed | tf_op | source)
XLA Modules:
  0.0 527.4 jit_solution(8425430569256399796)
XLA Ops:
  7.2 0.0 all-reduce.5.cloned.1.call-start
  7.2 28.5 %all_gather.10 = bf16[8,8192]{1,0:T(8,128)(2,1)S(1)} all-gather(bf16[8,1024]{1,0:T(8,128)(2,1)} %param.5), channel_id=1, replica_groups=mesh['row'=16,'col'=8,'vec'=2] {'col'}, dimensions={1}, use_global_device_ids=true | all-gather | bytes 147456 | tf_op jit(solution)/shard_map/all_gather | solution.py:16
  35.8 0.7 compare_select_fusion
  36.5 0.7 compare_and_fusion.1
  37.2 0.8 gather_fusion.1
  38.0 4.7 fusion
  42.7 0.4 copy.9
  43.8 0.6 convolution_bitcast_fusion
  44.5 0.2 copy.7
  44.7 1.1 copy.18
  45.8 0.0 all-reduce.5.cloned.1.call-update
  45.8 0.0 all-reduce.3.cloned.1.call-start
  45.9 20.7 %all_gather.9 = bf16[8,16384]{1,0:T(8,128)(2,1)S(1)} all-gather(bf16[8,1024]{1,0:T(8,128)(2,1)S(1)} %copy-done), channel_id=1, replica_groups=mesh['row'=16,'col'=8,'vec'=2] {'row'}, dimensions={1}, use_global_device_ids=true | all-gather | bytes 278528 | tf_op jit(solution)/shard_map/all_gather | solution.py:17
  66.6 0.8 gather_fusion
  67.4 6.8 %fusion.2 = f32[256,8,128]{2,1,0:T(8,128)S(1)} fusion(bf16[1,1,256,128,128]{4,3,2,1,0:T(8,128)(2,1)} %param.6, bf16[256,8,128]{2,1,0:T(8,128)(2,1)S(1)} %gather_fusion, pred[256]{0:T(512)(128)(4,1)S(1)} %get-tuple-element.2), kind=kOutput, calls=%fused_computation.4 | convolution fusion | flops 67371008 | bytes 9961728 | tf_op jit(solution)/shard_map/tij,vtj->vti/dot_general | solution.py:31
  74.2 0.6 convolution_bitcast_fusion.1
  74.8 0.9 copy.19
  75.7 5.9 %all_gather.11 = bf16[16,1024]{1,0:T(8,128)(2,1)S(1)} all-gather(bf16[8,1024]{1,0:T(8,128)(2,1)S(1)} %copy-done), channel_id=1, replica_groups=mesh['row'=16,'col'=8,'vec'=2] {'vec'}, dimensions={0}, use_global_device_ids=true | all-gather | bytes 49152 | tf_op jit(solution)/shard_map/all_gather | solution.py:50
  81.7 77.3 %all-reduce.5.cloned.1.call-done = f32[8,16384]{1,0:T(8,128)} async-done(((f32[8,16384]{1,0:T(8,128)}), f32[8,16384]{1,0:T(8,128)}) %all-reduce.5.cloned.1.call-update) | async-done | bytes 524304 | tf_op jit(solution)/shard_map/psum | solution.py:46
  159.0 79.9 %all-reduce.3.cloned.1.call-done = f32[8,8192]{1,0:T(8,128)} async-done(((f32[8,8192]{1,0:T(8,128)}), f32[8,8192]{1,0:T(8,128)}) %all-reduce.3.cloned.1.call-update) | async-done | bytes 262160 | tf_op jit(solution)/shard_map/psum | solution.py:45
  238.9 0.9 convolution_bitcast_fusion.2
  239.8 278.8 %psum.23 = f32[16,8]{0,1:T(8,128)S(1)} all-reduce(f32[16,8]{0,1:T(8,128)S(1)} %convolution_bitcast_fusion.2), channel_id=1, replica_groups=mesh['row'=16,'col'=8,'vec'=2] {'row','col'}, use_global_device_ids=true, to_apply=%region_2.3 | all-reduce | flops 128 | bytes 1024 | tf_op jit(solution)/shard_map/psum | solution.py:54
  518.6 0.6 broadcast_multiply_fusion
  519.2 1.4 fusion.25
  (12 shorter events, 0.1 us)
Async XLA Ops:
  7.2 36.6 %copy-start.1 = (s32[1,1,256]{2,1,0:T(1,128)S(1)}, s32[1,1,256]{2,1,0:T(1,128)}, u32[]{:S(2)}) copy-start(s32[1,1,256]{2,1,0:T(1,128)} %param.7) | copy-start | bytes 3076
  7.2 36.6 %copy-start.2 = (s32[1,1,256]{2,1,0:T(1,128)S(1)}, s32[1,1,256]{2,1,0:T(1,128)}, u32[]{:S(2)}) copy-start(s32[1,1,256]{2,1,0:T(1,128)} %param.8) | copy-start | bytes 3076
  7.2 151.8 %all-reduce.5.cloned.1.call-start = ((), (), s32[]{:S(2)}) async-start(), calls=%async_computation.1 | async-start | bytes 1048576 | tf_op jit(solution)/shard_map/psum | solution.py:46
  38.0 7.9 %copy-start = (bf16[8,1024]{1,0:T(8,128)(2,1)S(1)}, bf16[8,1024]{1,0:T(8,128)(2,1)}, u32[]{:S(2)}) copy-start(bf16[8,1024]{1,0:T(8,128)(2,1)} %param.5) | copy-start | bytes 49156
  45.8 193.1 %all-reduce.3.cloned.1.call-start = ((), (), s32[]{:S(2)}) async-start(), calls=%async_computation | async-start | bytes 524288 | tf_op jit(solution)/shard_map/psum | solution.py:45
Sparse Core Ops, SparseCore 0:
  45.9 113.0 all-reduce.4
  161.6 77.2 all-reduce.2
where the time goes:
time: 528 us; the launch traced here: 527 us
  blocking collectives  334 us (63%)
  waiting for transfers between devices  157 us (30%)
  between operations  14.8 us (3%)
  matrix products  13.7 us (3%)
    psum x1, blocking collectives, shards(): lax.psum(partial_gram, ('row', 'col')) / math.sqrt(width * nrow * ncol)  279 us
    psum x1, waiting for transfers between devices, shards(): row_whole = lax.psum(row_part, 'col')  79.9 us
    psum x1, waiting for transfers between devices, shards(): col_whole = lax.psum(col_part, 'row')  77.3 us
    all_gather x1, blocking collectives, shards(): row_x = lax.all_gather(vectors, 'col', axis=1, tiled=True)  28.5 us
    all_gather x1, blocking collectives, shards(): col_x = lax.all_gather(vectors, 'row', axis=1, tiled=True)  20.7 us
  transfers between devices with their start and end apart: 2, of which 2 were waited for; matrix products, arithmetic and copies ran while one was open for 2% of the time, Pallas kernels for 0%

commit v1 on v0

--- a/solution.py
+++ b/solution.py
@@ -13,7 +13,8 @@
     stretch = width // tile
     span = ncol * stretch
     colspan = nrow * stretch
-    row_x = lax.all_gather(vectors, "col", axis=1, tiled=True)
+    sent = jnp.stack([vectors] * lax.axis_size("col"))
+    row_x = jnp.concatenate(lax.all_to_all(sent, "col", 0, 0), axis=1)
     col_x = lax.all_gather(vectors, "row", axis=1, tiled=True)
     tiles = tile_vals[0, 0]
     rows = tile_rows[0, 0]

time: 528 us -> 527 us (level)
  blocking collectives: 334 us -> 304 us
  waiting for transfers between devices: 157 us -> 175 us
  starting transfers between devices: 0.08 us -> 5.8 us
    psum x1, waiting for transfers between devices: 77.3 us -> 115 us  [shards(): col_whole = lax.psum(col_part, 'row')]
    all_gather x1 -> x0, blocking collectives: 28.5 us -> none  [shards(): row_x = lax.all_gather(vectors, 'col', axis=1, tiled=True)]
    psum x1, waiting for transfers between devices: 79.9 us -> 60.8 us  [shards(): row_whole = lax.psum(row_part, 'col')]
    all_to_all x0 -> x1, starting transfers between devices: none -> 5.76 us  [shards(): row_x = jnp.concatenate(lax.all_to_all(sent, 'col', 0, 0), axis=1)]
  transfers between devices with their start and end apart: 2 -> 3, of which waited for: 2 -> 2; matrix products, arithmetic and copies ran while one was open for 2% -> 4% of each run, Pallas kernels for 0% -> 0%
where the time goes in v1:
time: 527 us; the launch traced here: 522 us
  blocking collectives  304 us (58%)
  waiting for transfers between devices  175 us (33%)
  between operations  14.8 us (3%)
  matrix products  14.1 us (3%)
  starting transfers between devices  5.8 us (1%)
    psum x1, blocking collectives, shards(): lax.psum(partial_gram, ('row', 'col')) / math.sqrt(width * nrow * ncol)  277 us
    psum x1, waiting for transfers between devices, shards(): col_whole = lax.psum(col_part, 'row')  115 us
    psum x1, waiting for transfers between devices, shards(): row_whole = lax.psum(row_part, 'col')  60.8 us
    all_gather x1, blocking collectives, shards(): col_x = lax.all_gather(vectors, 'row', axis=1, tiled=True)  20.9 us
  transfers between devices with their start and end apart: 3, of which 2 were waited for; matrix products, arithmetic and copies ran while one was open for 4% of the time, Pallas kernels for 0%

profile of v1, /device:TPU:8, one launch (start us, length us, event | category | flops | bytes accessed | tf_op | source)
XLA Modules:
  0.0 522.3 jit_solution(1593550357228074085)
XLA Ops:
  7.2 1.4 stack.2
  8.6 5.8 %all-to-all-start = ((bf16[8,8,1024]{2,1,0:T(8,128)(2,1)}), bf16[8,8,1024]{2,1,0:T(8,128)(2,1)S(1)}, u32[]{:S(2)}, u32[]{:S(2)}) async-start(bf16[8,8,1024]{2,1,0:T(8,128)(2,1)} %stack.2), calls=%async_computation | async-start | bytes 262144 | tf_op jit(solution)/shard_map/all_to_all | solution.py:17
  14.3 20.9 %all_gather.6 = bf16[8,16384]{1,0:T(8,128)(2,1)S(1)} all-gather(bf16[8,1024]{1,0:T(8,128)(2,1)} %param.5), channel_id=1, replica_groups=mesh['row'=16,'col'=8,'vec'=2] {'row'}, dimensions={1}, use_global_device_ids=true | all-gather | bytes 278528 | tf_op jit(solution)/shard_map/all_gather | solution.py:18
  35.9 0.7 compare_select_fusion.1
  36.6 0.8 gather_fusion
  37.4 0.7 compare_and_fusion.1
  38.1 6.8 %fusion.4 = f32[8,256,128]{2,0,1:T(8,128)S(1)} fusion(bf16[1,1,256,128,128]{4,3,2,1,0:T(8,128)(2,1)} %param.6, bf16[256,8,128]{2,1,0:T(8,128)(2,1)S(1)} %gather_fusion, pred[256]{0:T(512)(128)(4,1)S(1)} %get-tuple-element.8), kind=kOutput, calls=%fused_computation.6 | convolution fusion | flops 67371008 | bytes 9961728 | tf_op jit(solution)/shard_map/tij,vtj->vti/dot_general | solution.py:32
  45.0 0.6 convolution_bitcast_fusion.1
  45.6 0.9 copy.23
  46.4 0.0 all-reduce.3.cloned.1.call-update
  46.5 0.0 all-reduce.5.cloned.1.call-start
  46.6 0.8 gather_fusion.1
  47.4 4.7 fusion.7
  52.1 1.0 convolution_bitcast_fusion
  53.2 0.2 copy.13
  53.4 1.1 copy.22
  54.5 0.0 all-reduce.5.cloned.1.call-update
  54.5 6.0 %all_gather.7 = bf16[16,1024]{1,0:T(8,128)(2,1)S(1)} all-gather(bf16[8,1024]{1,0:T(8,128)(2,1)S(1)} %copy-done), channel_id=1, replica_groups=mesh['row'=16,'col'=8,'vec'=2] {'vec'}, dimensions={0}, use_global_device_ids=true | all-gather | bytes 49152 | tf_op jit(solution)/shard_map/all_gather | solution.py:51
  60.6 60.8 %all-reduce.3.cloned.1.call-done = f32[8,8192]{1,0:T(8,128)} async-done(((f32[8,8192]{1,0:T(8,128)}), f32[8,8192]{1,0:T(8,128)}) %all-reduce.3.cloned.1.call-update) | async-done | bytes 262160 | tf_op jit(solution)/shard_map/psum | solution.py:46
  121.4 114.5 %all-reduce.5.cloned.1.call-done = f32[8,16384]{1,0:T(8,128)} async-done(((f32[8,16384]{1,0:T(8,128)}), f32[8,16384]{1,0:T(8,128)}) %all-reduce.5.cloned.1.call-update) | async-done | bytes 524304 | tf_op jit(solution)/shard_map/psum | solution.py:47
  235.9 0.9 convolution_bitcast_fusion.2
  236.8 276.7 %psum.23 = f32[16,8]{0,1:T(8,128)S(1)} all-reduce(f32[16,8]{0,1:T(8,128)S(1)} %convolution_bitcast_fusion.2), channel_id=1, replica_groups=mesh['row'=16,'col'=8,'vec'=2] {'row','col'}, use_global_device_ids=true, to_apply=%region_2.3 | all-reduce | flops 128 | bytes 1024 | tf_op jit(solution)/shard_map/psum | solution.py:55
  513.5 0.6 broadcast_multiply_fusion
  514.1 1.4 fusion.30
  (10 shorter events, 0.0 us)
Async XLA Ops:
  7.2 39.4 %copy-start.1 = (s32[1,1,256]{2,1,0:T(1,128)S(1)}, s32[1,1,256]{2,1,0:T(1,128)}, u32[]{:S(2)}) copy-start(s32[1,1,256]{2,1,0:T(1,128)} %param.7) | copy-start | bytes 3076
  8.6 38.0 %all-to-all-start = ((bf16[8,8,1024]{2,1,0:T(8,128)(2,1)}), bf16[8,8,1024]{2,1,0:T(8,128)(2,1)S(1)}, u32[]{:S(2)}, u32[]{:S(2)}) async-start(bf16[8,8,1024]{2,1,0:T(8,128)(2,1)} %stack.2), calls=%async_computation | async-start | bytes 262144 | tf_op jit(solution)/shard_map/all_to_all | solution.py:17
  14.3 107.1 %all-reduce.3.cloned.1.call-start = ((), (), s32[]{:S(2)}) async-start(), calls=%async_computation.1 | async-start | bytes 524288 | tf_op jit(solution)/shard_map/psum | solution.py:46
  45.0 9.6 %copy-start = (bf16[8,1024]{1,0:T(8,128)(2,1)S(1)}, bf16[8,1024]{1,0:T(8,128)(2,1)}, u32[]{:S(2)}) copy-start(bf16[8,1024]{1,0:T(8,128)(2,1)} %param.5) | copy-start | bytes 49156
  46.5 189.4 %all-reduce.5.cloned.1.call-start = ((), (), s32[]{:S(2)}) async-start(), calls=%async_computation.2 | async-start | bytes 1048576 | tf_op jit(solution)/shard_map/psum | solution.py:47
Sparse Core Ops, SparseCore 0:
  46.6 74.7 all-reduce.2
  123.7 112.1 all-reduce.4
